TPU v7x, 32 devices: a whole 2x2x4 slice. The times are simulated.
32 devices in a mesh: row: 4 (over y, x), col: 8 (over z, core).
Axes of the slice: x: 2, y: 2, z: 4, core: 2. Of those that a mesh axis runs over, the one named last changes fastest.
Arguments:
- tokens: bfloat16 [294912, 1024], P(('row', 'col')), may hold values from -6 to 6
- router_weight: bfloat16 [1024], P(('row', 'col')), may hold values from -0.1875 to 0.1875
- norm_first: bfloat16 [1024], P(('row', 'col')), may hold values from 0.099609375 to 1.8984375
- qkv_weight: bfloat16 [1024, 3072], P('row', 'col'), may hold values from -0.1875 to 0.1875
- out_weight: bfloat16 [1024, 1024], P('col', 'row'), may hold values from -0.75 to 0.75
- norm_second: bfloat16 [1024], P(('row', 'col')), may hold values from 0.099609375 to 1.8984375
- up_weight: bfloat16 [1024, 4096], P('row', 'col'), may hold values from -0.1875 to 0.1875
- down_weight: bfloat16 [4096, 1024], P('col', 'row'), may hold values from -0.09375 to 0.09375
- route_index: int32 [288, 128], P(('row', 'col')), may hold values from 0 to 1023, as said below
- out_cotangent: bfloat16 [294912, 1024], P(('row', 'col')), may hold values from -6 to 6
Outputs:
- output: bfloat16 [294912, 1024], P(('row', 'col'))
- input_grad: float32 [294912, 1024], P(('row', 'col'))
- router_grad: float32 [1024], P(('row', 'col'))
- norm_first_grad: float32 [1024], P(('row', 'col'))
- qkv_grad: float32 [1024, 3072], P('row', 'col')
- out_grad: float32 [1024, 1024], P('col', 'row')
- norm_second_grad: float32 [1024], P(('row', 'col'))
- up_grad: float32 [1024, 4096], P('row', 'col')
- down_grad: float32 [4096, 1024], P('col', 'row')
Inputs may be any that keep to these rules, and one draw needn't show every extreme that they name: `route_index`: each row lists 128 distinct positions of one sequence in increasing order; the first is 0 and the last 1023.
All inputs are finite; a program needn't handle non-finite values.
Results may differ from a plain program's by a relative error of at most 0.019.
Values may be sent and summed in bfloat16 or wider, within the bound.
No kernel may reach another device: no remote copies, remote signals or barrier semaphores. Data moves between devices by JAX's collectives and lax.ppermute only.
A program may use at most 320 MiB of HBM per device.

v0:
```python
import jax
import jax.numpy as jnp
from jax import lax
from jax.sharding import PartitionSpec as P

HEADS = 16
HD = 64
epsilon = 1e-06


def local(
    tokens,
    router_weight,
    norm_first,
    qkv_weight,
    out_weight,
    norm_second,
    up_weight,
    down_weight,
    route_index,
    out_cotangent,
):
    seq_local, routed = route_index.shape
    seq_length = tokens.shape[0] // seq_local
    width = tokens.shape[1]
    starts = jnp.arange(seq_local, dtype=jnp.int32) * seq_length
    token_rows = (route_index + starts[:, None]).reshape(-1)
    row_count = token_rows.shape[0]
    col_pieces = (
        lax.all_gather(qkv_weight, "col", axis=1, tiled=True),
        lax.all_gather(out_weight, "col", axis=0, tiled=True),
        lax.all_gather(up_weight, "col", axis=1, tiled=True),
        lax.all_gather(down_weight, "col", axis=0, tiled=True),
        lax.all_gather(norm_first, "col", axis=0, tiled=True),
        lax.all_gather(norm_second, "col", axis=0, tiled=True),
        lax.all_gather(router_weight, "col", axis=0, tiled=True),
    )
    gathered = (
        lax.all_gather(col_pieces[0], "row", axis=0, tiled=True),
        lax.all_gather(col_pieces[1], "row", axis=1, tiled=True),
        lax.all_gather(col_pieces[2], "row", axis=0, tiled=True),
        lax.all_gather(col_pieces[3], "row", axis=1, tiled=True),
        lax.all_gather(col_pieces[4], "row", axis=0, tiled=True),
        lax.all_gather(col_pieces[5], "row", axis=0, tiled=True),
        lax.all_gather(col_pieces[6], "row", axis=0, tiled=True),
    )
    w_qkv, w_out, w_up, w_down, first_full, second_full, router_full = gathered
    first_gain = first_full.astype(jnp.float32)
    second_gain = second_full.astype(jnp.float32)
    router_vec = router_full.astype(jnp.float32)
    picked_full = tokens[token_rows]
    h_full = picked_full.astype(jnp.float32)
    gate_value = jax.nn.sigmoid(
        jnp.dot(picked_full, router_full, preferred_element_type=jnp.float32)
    )
    inverse_first = lax.rsqrt(jnp.mean(h_full * h_full, axis=-1, keepdims=True) + epsilon)
    normed = (h_full * inverse_first * first_gain).astype(jnp.bfloat16)
    projected = jnp.dot(normed, w_qkv, preferred_element_type=jnp.float32).astype(jnp.bfloat16)
    heads_qkv = projected.reshape(seq_local, routed, HEADS, 3, HD)
    queries = heads_qkv[:, :, :, 0]
    key_rows = heads_qkv[:, :, :, 1]
    values = heads_qkv[:, :, :, 2]
    scaling = HD ** (-0.5)
    places = jnp.arange(routed, dtype=jnp.int32)
    causal = places[:, None] >= places[None, :]
    scores = (
        jnp.einsum("sqhe,skhe->shqk", queries, key_rows, preferred_element_type=jnp.float32)
        * scaling
    )
    scores = jnp.where(causal, scores, -1e30)
    highest = jnp.max(scores, axis=-1, keepdims=True)
    expanded = jnp.exp(scores - highest)
    totals = jnp.sum(expanded, axis=-1, keepdims=True)
    attn_probs = (expanded / totals).astype(jnp.bfloat16)
    log_total = highest + jnp.log(totals)
    mixed = jnp.einsum("shqk,skhe->sqhe", attn_probs, values, preferred_element_type=jnp.float32)
    context = mixed.reshape(row_count, width).astype(jnp.bfloat16)
    attn_out = jnp.dot(context, w_out, preferred_element_type=jnp.float32)
    middle = h_full + attn_out
    inverse_mid = lax.rsqrt(jnp.mean(middle * middle, axis=-1, keepdims=True) + epsilon)
    normed_mid = (middle * inverse_mid * second_gain).astype(jnp.bfloat16)
    pre_act = jnp.dot(normed_mid, w_up, preferred_element_type=jnp.float32)
    activated, gelu_back = jax.vjp(jax.nn.gelu, pre_act)
    hidden = activated.astype(jnp.bfloat16)
    mlp_out = jnp.dot(hidden, w_down, preferred_element_type=jnp.float32)
    branch = attn_out + mlp_out
    output = (
        tokens.astype(jnp.float32)
        .at[token_rows]
        .add(gate_value[:, None] * branch)
        .astype(jnp.bfloat16)
    )
    back_pieces = (
        lax.all_gather(qkv_weight, "col", axis=1, tiled=True),
        lax.all_gather(out_weight, "col", axis=0, tiled=True),
        lax.all_gather(up_weight, "col", axis=1, tiled=True),
        lax.all_gather(down_weight, "col", axis=0, tiled=True),
    )
    w_qkv, w_out, w_up, w_down = (
        lax.all_gather(back_pieces[0], "row", axis=0, tiled=True),
        lax.all_gather(back_pieces[1], "row", axis=1, tiled=True),
        lax.all_gather(back_pieces[2], "row", axis=0, tiled=True),
        lax.all_gather(back_pieces[3], "row", axis=1, tiled=True),
    )
    grad_out = out_cotangent.astype(jnp.float32)
    grad_rows = grad_out[token_rows]
    gate_grad = jnp.sum(grad_rows * branch, axis=-1)
    grad_branch = gate_value[:, None] * grad_rows
    grad_mlp = grad_branch.astype(jnp.bfloat16)
    grad_hidden = jnp.dot(grad_mlp, w_down.T, preferred_element_type=jnp.float32)
    down_part = jnp.dot(hidden.T, grad_mlp, preferred_element_type=jnp.float32)
    grad_pre = gelu_back(grad_hidden)[0].astype(jnp.bfloat16)
    up_part = jnp.dot(normed_mid.T, grad_pre, preferred_element_type=jnp.float32)
    grad_normed_mid = jnp.dot(grad_pre, w_up.T, preferred_element_type=jnp.float32)
    second_part = jnp.sum(grad_normed_mid * middle * inverse_mid, axis=0)
    grad_scaled_mid = grad_normed_mid * second_gain
    mid_sum = jnp.sum(grad_scaled_mid * middle, axis=-1, keepdims=True)
    grad_middle = inverse_mid * grad_scaled_mid - middle * inverse_mid**3 * mid_sum / width
    grad_attn = (grad_branch + grad_middle).astype(jnp.bfloat16)
    grad_context = jnp.dot(grad_attn, w_out.T, preferred_element_type=jnp.float32).astype(
        jnp.bfloat16
    )
    out_part = jnp.dot(context.T, grad_attn, preferred_element_type=jnp.float32)
    grad_heads = grad_context.reshape(seq_local, routed, HEADS, HD)
    again = (
        jnp.einsum("sqhe,skhe->shqk", queries, key_rows, preferred_element_type=jnp.float32)
        * scaling
    )
    again = jnp.where(causal, again, -1e30)
    probs_exact = jnp.exp(again - log_total)
    grad_probs = jnp.einsum(
        "sqhe,skhe->shqk", grad_heads, values, preferred_element_type=jnp.float32
    )
    inner_sum = jnp.sum(grad_probs * probs_exact, axis=-1, keepdims=True)
    grad_scores = (probs_exact * (grad_probs - inner_sum)).astype(jnp.bfloat16)
    grad_query = (
        jnp.einsum("shqk,skhe->sqhe", grad_scores, key_rows, preferred_element_type=jnp.float32)
        * scaling
    )
    grad_key = (
        jnp.einsum("shqk,sqhe->skhe", grad_scores, queries, preferred_element_type=jnp.float32)
        * scaling
    )
    grad_value = jnp.einsum(
        "shqk,sqhe->skhe", attn_probs, grad_heads, preferred_element_type=jnp.float32
    )
    grad_projected = (
        jnp.stack([grad_query, grad_key, grad_value], axis=3)
        .reshape(row_count, 3 * width)
        .astype(jnp.bfloat16)
    )
    qkv_part = jnp.dot(normed.T, grad_projected, preferred_element_type=jnp.float32)
    grad_normed = jnp.dot(grad_projected, w_qkv.T, preferred_element_type=jnp.float32)
    first_part = jnp.sum(grad_normed * h_full * inverse_first, axis=0)
    grad_scaled_first = grad_normed * first_gain
    first_sum = jnp.sum(grad_scaled_first * h_full, axis=-1, keepdims=True)
    grad_norm_in = inverse_first * grad_scaled_first - h_full * inverse_first**3 * first_sum / width
    grad_logit = gate_grad * gate_value * (1.0 - gate_value)
    router_part = jnp.sum(grad_logit[:, None] * h_full, axis=0)
    grad_picked = grad_middle + grad_norm_in + grad_logit[:, None] * router_vec
    input_grad = grad_out.at[token_rows].add(grad_picked)
    all_pieces = (
        lax.psum_scatter(
            qkv_part.astype(jnp.bfloat16), "row", scatter_dimension=0, tiled=True
        ).astype(jnp.float32),
        lax.psum_scatter(
            out_part.astype(jnp.bfloat16), "row", scatter_dimension=1, tiled=True
        ).astype(jnp.float32),
        lax.psum_scatter(
            up_part.astype(jnp.bfloat16), "row", scatter_dimension=0, tiled=True
        ).astype(jnp.float32),
        lax.psum_scatter(
            down_part.astype(jnp.bfloat16), "row", scatter_dimension=1, tiled=True
        ).astype(jnp.float32),
        lax.psum_scatter(
            first_part.astype(jnp.bfloat16), "row", scatter_dimension=0, tiled=True
        ).astype(jnp.float32),
        lax.psum_scatter(
            second_part.astype(jnp.bfloat16), "row", scatter_dimension=0, tiled=True
        ).astype(jnp.float32),
        lax.psum_scatter(
            router_part.astype(jnp.bfloat16), "row", scatter_dimension=0, tiled=True
        ).astype(jnp.float32),
    )
    summed = (
        lax.psum_scatter(
            all_pieces[0].astype(jnp.bfloat16), "col", scatter_dimension=1, tiled=True
        ).astype(jnp.float32),
        lax.psum_scatter(
            all_pieces[1].astype(jnp.bfloat16), "col", scatter_dimension=0, tiled=True
        ).astype(jnp.float32),
        lax.psum_scatter(
            all_pieces[2].astype(jnp.bfloat16), "col", scatter_dimension=1, tiled=True
        ).astype(jnp.float32),
        lax.psum_scatter(
            all_pieces[3].astype(jnp.bfloat16), "col", scatter_dimension=0, tiled=True
        ).astype(jnp.float32),
        lax.psum_scatter(
            all_pieces[4].astype(jnp.bfloat16), "col", scatter_dimension=0, tiled=True
        ).astype(jnp.float32),
        lax.psum_scatter(
            all_pieces[5].astype(jnp.bfloat16), "col", scatter_dimension=0, tiled=True
        ).astype(jnp.float32),
        lax.psum_scatter(
            all_pieces[6].astype(jnp.bfloat16), "col", scatter_dimension=0, tiled=True
        ).astype(jnp.float32),
    )
    qkv_grad, out_grad, up_grad, down_grad, norm_first_grad, norm_second_grad, router_grad = summed
    return (
        output,
        input_grad,
        router_grad,
        norm_first_grad,
        qkv_grad,
        out_grad,
        norm_second_grad,
        up_grad,
        down_grad,
    )


def solution(mesh):
    placed = (
        P(("row", "col"), None),
        P(("row", "col")),
        P(("row", "col")),
        P("row", "col"),
        P("col", "row"),
        P(("row", "col")),
        P("row", "col"),
        P("col", "row"),
        P(("row", "col"), None),
        P(("row", "col"), None),
    )
    return jax.shard_map(
        local,
        mesh=mesh,
        in_specs=placed,
        out_specs=(
            P(("row", "col"), None),
            P(("row", "col"), None),
            P(("row", "col")),
            P(("row", "col")),
            P("row", "col"),
            P("col", "row"),
            P(("row", "col")),
            P("row", "col"),
            P("col", "row"),
        ),
        check_vma=False,
    )
```

profile of v0, /device:TPU:0, one launch (start us, length us, event | category | flops | bytes accessed | tf_op | source)
XLA Modules:
  0.0 964.3 jit_solution(17025223967984651840)
XLA Ops:
  9.5 28.1 %all-gather.11.cloned.1.call-done = bf16[256,3072]{1,0:T(8,128)(2,1)} async-done(((bf16[256,384]{1,0:T(8,128)(2,1)}), bf16[256,3072]{1,0:T(8,128)(2,1)}) %all-gather.11.cloned.1.call-update) | async-done | bytes 1572880 | tf_op jit(solution)/shard_map/all_gather | solution.py:30
  37.7 16.9 %all_gather.56 = bf16[1024,256]{1,0:T(8,128)(2,1)} all-gather(bf16[128,256]{1,0:T(8,128)(2,1)} %param.14), channel_id=1, replica_groups=mesh['row'=4,'col'=8] {'col'}, dimensions={0}, use_global_device_ids=true | all-gather | bytes 589824 | tf_op jit(solution)/shard_map/all_gather | solution.py:31
  102.9 16.6 %gather_fusion = bf16[1152,1024]{1,0:T(8,128)(2,1)} fusion(bf16[9216,1024]{1,0:T(8,128)(2,1)} %param.10, s32[2048]{0:T(1024)S(1)} %pad_clamp_fusion), kind=kCustom, calls=%fused_computation | custom fusion | bytes 4723200 | tf_op jit(solution)/shard_map/gather | solution.py:51
  122.5 21.7 %convert_element_type.133 = f32[9216,1024]{1,0:T(8,128)} convert(bf16[9216,1024]{1,0:T(8,128)(2,1)} %param.19) | non-fusion elementwise | flops 9437184 | bytes 56623104 | tf_op jit(solution)/shard_map/convert_element_type | solution.py:105
  144.2 18.3 %gather_fusion.1 = f32[1152,1024]{1,0:T(8,128)} fusion(f32[9216,1024]{1,0:T(8,128)} %convert_element_type.133, s32[2048]{0:T(1024)S(1)} %pad_clamp_fusion), kind=kCustom, calls=%fused_computation.1 | custom fusion | bytes 9441792 | tf_op jit(solution)/shard_map/gather | solution.py:106
  192.1 30.3 %reshape.178 = bf16[9,128,16,3,64]{4,3,2,1,0:T(4,128)(2,1)} reshape(bf16[1152,3072]{1,0:T(8,128)(2,1)} %convolution_convert_fusion) | data formatting | bytes 14155776 | tf_op jit(solution)/shard_map/reshape | solution.py:59
  222.4 35.7 %fusion.63 = (bf16[9,128,16,1,64]{4,3,2,1,0:T(2,128)(2,1)}, bf16[9,128,16,1,64]{4,3,2,1,0:T(2,128)(2,1)}, bf16[9,128,16,1,64]{4,3,2,1,0:T(2,128)(2,1)}) fusion(bf16[9,128,16,3,64]{4,3,2,1,0:T(4,128)(2,1)} %reshape.178), kind=kLoop, calls=%fused_computation.106 | loop fusion | bytes 14155776 | tf_op jit(solution)/shard_map/slice | solution.py:62
  258.1 18.9 %copy.91 = bf16[9,128,16,1,64]{1,4,2,0,3:T(8,128)(2,1)S(1)} copy(bf16[9,128,16,1,64]{4,3,2,1,0:T(2,128)(2,1)} %get-tuple-element.25) | data formatting | bytes 4718592
  277.0 20.0 %copy.92 = bf16[9,128,16,1,64]{1,4,2,0,3:T(8,128)(2,1)} copy(bf16[9,128,16,1,64]{4,3,2,1,0:T(2,128)(2,1)} %get-tuple-element.26) | data formatting | bytes 4718592
  297.0 20.3 %copy.93 = bf16[9,128,16,1,64]{1,4,2,0,3:T(8,128)(2,1)} copy(bf16[9,128,16,1,64]{4,3,2,1,0:T(2,128)(2,1)} %get-tuple-element.27) | data formatting | bytes 4718592
  345.1 18.2 %fusion.62 = f32[1152,4096]{1,0:T(8,128)} fusion(bf16[1024,4096]{1,0:T(8,128)(2,1)} %all-gather.19.cloned.1.call-done, f32[1152,1024]{0,1:T(8,128)} %get-tuple-element.24, f32[1024]{0:T(1024)S(1)} %bitcast.110, f32[1152]{0:T(1024)S(1)} %get-tuple-element.34), kind=kOutput, calls=%fused_computation.105 | convolution fusion | flops 9667215360 | bytes 31990272 | tf_op jit(solution)/shard_map/dot_general | solution.py:82
  363.3 22.6 %all-gather.23.cloned.1.call-done = bf16[4096,1024]{1,0:T(8,128)(2,1)} async-done(((bf16[4096,256]{1,0:T(8,128)(2,1)}), bf16[4096,1024]{1,0:T(8,128)(2,1)}) %all-gather.23.cloned.1.call-update) | async-done | bytes 8388624 | tf_op jit(solution)/shard_map/all_gather | solution.py:42
  385.9 28.3 %fusion.6 = bf16[1152,4096]{1,0:T(8,128)(2,1)} fusion(f32[1152,4096]{1,0:T(8,128)} %fusion.62, bf16[4096,1024]{1,0:T(8,128)(2,1)} %all-gather.23.cloned.1.call-done, f32[1152,1024]{0,1:T(8,128)} %copy.65, f32[1152]{0:T(1024)S(1)} %add_divide_fusion), kind=kOutput, calls=%fused_computation.12 | convolution fusion | flops 9760407552 | bytes 41423360 | tf_op jit(solution)/shard_map/dot_general | solution.py:110
  414.1 19.3 %multiply_reduce_fusion.1 = (bf16[1024]{0:T(1024)(128)(2,1)}, f32[1152]{0:T(1024)S(1)}, f32[1152,1024]{0,1:T(8,128)}) fusion(f32[1152,1024]{0,1:T(8,128)} %get-tuple-element.24, f32[1152]{0:T(1024)S(1)} %get-tuple-element.34, f32[1024]{0:T(1024)S(1)} %bitcast.111, bf16[1152,4096]{1,0:T(8,128)(2,1)} %fusion.6, ...), kind=kOutput, calls=%fused_computation.50 | convolution fusion | flops 9670752256 | bytes 27278336 | tf_op jit(solution)/shard_map/dot_general | solution.py:114
  433.4 26.0 %multiply_reduce_fusion.2 = (f32[1152]{0:T(1024)}, f32[1152,1024]{0,1:T(8,128)}, bf16[1152,1024]{0,1:T(8,128)(2,1)}) fusion(f32[1152,1024]{0,1:T(8,128)} %copy.65, f32[1152]{0:T(1024)S(1)} %add_divide_fusion, f32[1152]{0:T(1024)S(1)} %get-tuple-element.10, f32[1152,1024]{0,1:T(8,128)} %get-tuple-element.24, f32[1152]{0:T(1024)S(1)} %get-tuple-element.33, ...), kind=kOutput, calls=%fused_computation.51 | convolution fusion | flops 9721478144 | bytes 53242368 | tf_op jit(solution)/shard_map/dot_general | solution.py:85
  547.6 21.4 %convolution_convert_fusion.1 = bf16[4096,1024]{1,0:T(8,128)(2,1)} fusion(f32[1152,1024]{0,1:T(8,128)} %copy.65, f32[1152]{0:T(1024)S(1)} %add_divide_fusion, f32[1152,4096]{1,0:T(8,128)} %fusion.62), kind=kOutput, calls=%fused_computation.29 | convolution fusion | flops 9712697344 | bytes 31986176 | tf_op jit(solution)/shard_map/dot_general | solution.py:111
  569.1 18.3 %convolution_convert_fusion.2 = bf16[1024,4096]{1,0:T(8,128)(2,1)} fusion(bf16[1152,4096]{1,0:T(8,128)(2,1)} %fusion.6, f32[1152,1024]{0,1:T(8,128)} %get-tuple-element.24, f32[1024]{0:T(1024)S(1)} %bitcast.113, f32[1152]{0:T(1024)S(1)} %get-tuple-element.34), kind=kOutput, calls=%fused_computation.30 | convolution fusion | flops 9671409664 | bytes 22553088 | tf_op jit(solution)/shard_map/dot_general | solution.py:113
  588.0 29.9 %reduce-scatter.11.cloned.1.call-done = bf16[256,3072]{1,0:T(8,128)(2,1)} async-done(((bf16[1024,3072]{1,0:T(8,128)(2,1)}), bf16[256,3072]{1,0:T(8,128)(2,1)}) %reduce-scatter.11.cloned.1.call-update) | async-done | bytes 1572880 | tf_op jit(solution)/shard_map/reduce_scatter | solution.py:163
  620.6 86.9 %reduce-scatter.21.cloned.1.call-done = bf16[4096,256]{1,0:T(8,128)(2,1)} async-done(((bf16[4096,1024]{1,0:T(8,128)(2,1)}), bf16[4096,256]{1,0:T(8,128)(2,1)}) %reduce-scatter.21.cloned.1.call-update) | async-done | bytes 2097168 | tf_op jit(solution)/shard_map/reduce_scatter | solution.py:172
  707.7 21.3 %convert_element_type.120 = f32[9216,1024]{1,0:T(8,128)} convert(bf16[9216,1024]{1,0:T(8,128)(2,1)} %param.10) | non-fusion elementwise | flops 9437184 | bytes 56623104 | tf_op jit(solution)/shard_map/convert_element_type | solution.py:88
  737.0 60.6 %reduce-scatter.17.cloned.1.call-done = bf16[256,4096]{1,0:T(8,128)(2,1)} async-done(((bf16[1024,4096]{1,0:T(8,128)(2,1)}), bf16[256,4096]{1,0:T(8,128)(2,1)}) %reduce-scatter.17.cloned.1.call-update) | async-done | bytes 2097168 | tf_op jit(solution)/shard_map/reduce_scatter | solution.py:169
  825.7 39.5 %scatter_fusion.1 = f32[9216,1024]{1,0:T(8,128)} fusion(f32[9216,1024]{1,0:T(8,128)} %convert_element_type.133, s32[1152]{0:T(1024)S(1)} %copy-done.11, f32[1152,1024]{1,0:T(8,128)} %copy.76), kind=kCustom, calls=%fused_computation.3 | custom fusion | flops 1179648 | bytes 14160384 | tf_op jit(solution)/shard_map/scatter-add | solution.py:161
  874.8 39.4 %scatter_fusion = f32[9216,1024]{1,0:T(8,128)} fusion(f32[9216,1024]{1,0:T(8,128)} %convert_element_type.120, s32[1152]{0:T(1024)S(1)} %copy-done.11, f32[1152,1024]{1,0:T(8,128)} %copy.64), kind=kCustom, calls=%fused_computation.2 | custom fusion | flops 1179648 | bytes 14160384 | tf_op jit(solution)/shard_map/scatter-add | solution.py:90
  914.1 20.9 %convert_element_type.132 = bf16[9216,1024]{1,0:T(8,128)(2,1)} convert(f32[9216,1024]{1,0:T(8,128)} %scatter_fusion) | non-fusion elementwise | flops 9437184 | bytes 56623104 | tf_op jit(solution)/shard_map/convert_element_type | solution.py:91
  (176 shorter events, 268.1 us)
Async XLA Ops:
  7.2 61.8 %copy-start.28 = (u32[32]{0:T(128)S(1)}, u32[32]{0:T(128)}, u32[]{:S(2)}) copy-start(u32[32]{0:T(128)} %constant.40) | copy-start | bytes 388
  7.2 63.0 %copy-start.29 = (bf16[32]{0:T(256)(128)(2,1)S(1)}, bf16[32]{0:T(256)(128)(2,1)}, u32[]{:S(2)}) copy-start(bf16[32]{0:T(256)(128)(2,1)} %param.15) | copy-start | bytes 196
  7.2 63.3 %copy-start.30 = (bf16[32]{0:T(256)(128)(2,1)S(1)}, bf16[32]{0:T(256)(128)(2,1)}, u32[]{:S(2)}) copy-start(bf16[32]{0:T(256)(128)(2,1)} %param.12) | copy-start | bytes 196
  7.2 63.5 %copy-start.31 = (bf16[32]{0:T(256)(128)(2,1)S(1)}, bf16[32]{0:T(256)(128)(2,1)}, u32[]{:S(2)}) copy-start(bf16[32]{0:T(256)(128)(2,1)} %param.11) | copy-start | bytes 196
  7.2 95.0 %copy-start.26 = (s32[9,128]{1,0:T(8,128)S(1)}, s32[9,128]{1,0:T(8,128)}, u32[]{:S(2)}) copy-start(s32[9,128]{1,0:T(8,128)} %param.18) | copy-start | bytes 13828
  7.2 30.4 %all-gather.11.cloned.1.call-start = ((), (), s32[]{:S(2)}) async-start(), calls=%async_computation.8 | async-start | bytes 1769472 | tf_op jit(solution)/shard_map/all_gather | solution.py:30
  8.0 60.9 %all-gather.17.cloned.1.call-start = ((), (), s32[]{:S(2)}) async-start(), calls=%async_computation.11 | async-start | bytes 2359296 | tf_op jit(solution)/shard_map/all_gather | solution.py:32
  8.7 169.6 %all-gather.21.cloned.1.call-start = ((), (), s32[]{:S(2)}) async-start(), calls=%async_computation.13 | async-start | bytes 2359296 | tf_op jit(solution)/shard_map/all_gather | solution.py:33
  9.4 169.8 %all-gather.13.cloned.1.call-start = ((), (), s32[]{:S(2)}) async-start(), calls=%async_computation.9 | async-start | bytes 7864320 | tf_op jit(solution)/shard_map/all_gather | solution.py:39
  37.7 297.0 %all-gather.15.cloned.1.call-start = ((), (), s32[]{:S(2)}) async-start(), calls=%async_computation.10 | async-start | bytes 2621440 | tf_op jit(solution)/shard_map/all_gather | solution.py:40
  54.7 290.4 %all-gather.19.cloned.1.call-start = ((), (), s32[]{:S(2)}) async-start(), calls=%async_computation.12 | async-start | bytes 10485760 | tf_op jit(solution)/shard_map/all_gather | solution.py:41
  68.9 317.0 %all-gather.23.cloned.1.call-start = ((), (), s32[]{:S(2)}) async-start(), calls=%async_computation.14 | async-start | bytes 10485760 | tf_op jit(solution)/shard_map/all_gather | solution.py:42
  102.2 77.1 %copy-start.21 = (f32[4,1,256]{2,1,0:T(1,128)}, f32[4,1,256]{2,1,0:T(1,128)S(1)}, u32[]{:S(2)}) copy-start(f32[4,1,256]{2,1,0:T(1,128)S(1)} %convert_element_type.155) | copy-start | bytes 12292
  178.4 409.1 %reduce-scatter.13.cloned.1.call-start = ((), (), s32[]{:S(2)}) async-start(), calls=%async_computation.16 | async-start | bytes 2621440 | tf_op jit(solution)/shard_map/reduce_scatter | solution.py:166
  345.0 88.4 %copy-start.19 = (f32[1152]{0:T(1024)}, f32[1152]{0:T(1024)S(1)}, u32[]{:S(2)}) copy-start(f32[1152]{0:T(1024)S(1)} %get-tuple-element.33) | copy-start | bytes 13828
  466.6 151.3 %reduce-scatter.11.cloned.1.call-start = ((), (), s32[]{:S(2)}) async-start(), calls=%async_computation.15 | async-start | bytes 7864320 | tf_op jit(solution)/shard_map/reduce_scatter | solution.py:163
  547.6 160.0 %reduce-scatter.21.cloned.1.call-start = ((), (), s32[]{:S(2)}) async-start(), calls=%async_computation.20 | async-start | bytes 10485760 | tf_op jit(solution)/shard_map/reduce_scatter | solution.py:172
  569.1 228.6 %reduce-scatter.17.cloned.1.call-start = ((), (), s32[]{:S(2)}) async-start(), calls=%async_computation.18 | async-start | bytes 10485760 | tf_op jit(solution)/shard_map/reduce_scatter | solution.py:169
  587.4 363.0 %reduce-scatter.15.cloned.1.call-start = ((), (), s32[]{:S(2)}) async-start(), calls=%async_computation.17 | async-start | bytes 589824 | tf_op jit(solution)/shard_map/reduce_scatter | solution.py:189
  588.0 363.9 %reduce-scatter.25.cloned.1.call-start = ((), (), s32[]{:S(2)}) async-start(), calls=%async_computation.22 | async-start | bytes 1769472
  620.6 333.2 %reduce-scatter.23.cloned.1.call-start = ((), (), s32[]{:S(2)}) async-start(), calls=%async_computation.21 | async-start | bytes 2359296 | tf_op jit(solution)/shard_map/reduce_scatter | solution.py:195
  707.6 247.9 %reduce-scatter.19.cloned.1.call-start = ((), (), s32[]{:S(2)}) async-start(), calls=%async_computation.19 | async-start | bytes 2359296 | tf_op jit(solution)/shard_map/reduce_scatter | solution.py:192
  730.9 66.7 %copy-start.13 = (f32[1152]{0:T(1024)S(1)}, f32[1152]{0:T(1024)}, u32[]{:S(2)}) copy-start(f32[1152]{0:T(1024)} %copy-done.12) | copy-start | bytes 13828
  730.9 66.7 %copy-start.25 = (f32[1152]{0:T(1024)S(1)}, f32[1152]{0:T(1024)}, u32[]{:S(2)}) copy-start(f32[1152]{0:T(1024)} %get-tuple-element.28) | copy-start | bytes 13828
  (24 other events, 345.2 us)
Sparse Core Ops, SparseCore 0:
  9.7 27.9 all-gather.10
  39.2 29.5 all-gather.16
  70.5 28.3 all-gather.20
  100.6 69.6 all-gather.12
  172.0 35.1 all-gather.14
  208.9 87.6 all-gather.18
  298.4 87.4 all-gather.22
  466.8 35.1 reduce-scatter.12
  547.7 70.2 reduce-scatter.10
  621.2 86.3 reduce-scatter.20
  711.2 86.3 reduce-scatter.16
  799.8 30.9 reduce-scatter.14
  833.1 32.4 reduce-scatter.24
  867.7 33.6 reduce-scatter.22
  903.5 34.3 reduce-scatter.18
where the time goes:
time: 975 us; the launch traced here: 964 us
  waiting for transfers between devices  245 us (25%)
  matrix products  226 us (23%)
  local copies, waits for them, and re-layouts  221 us (23%)
  other arithmetic  176 us (18%)
  blocking collectives  78.4 us (8%)
  between operations  16.9 us (2%)
    reduce_scatter x1, waiting for transfers between devices, local(): lax.psum_scatter(down_part.astype(jnp.bfloat16), 'row', scatter_dimension...  86.9 us
    unnamed x86, local copies, waits for them, and re-layouts  70.9 us
    reduce_scatter x1, waiting for transfers between devices, local(): lax.psum_scatter(up_part.astype(jnp.bfloat16), 'row', scatter_dimension=0...  60.6 us
    scatter-add x1, other arithmetic, local(): input_grad = grad_out.at[token_rows].add(grad_picked)  39.5 us
    scatter-add x1, other arithmetic, local(): output = tokens.astype(jnp.float32).at[token_rows].add(gate_value[:, None...  39.4 us
    unnamed x3, blocking collectives  38.8 us
    slice x1, local copies, waits for them, and re-layouts, local(): values = heads_qkv[:, :, :, 2]  35.7 us
    reshape x1, local copies, waits for them, and re-layouts, local(): heads_qkv = projected.reshape(seq_local, routed, HEADS, 3, HD)  30.3 us
  transfers between devices with their start and end apart: 15, of which 6 were waited for; matrix products, arithmetic and copies ran while one was open for 55% of the time, Pallas kernels for 0%

commit v1 on v0

--- a/solution.py
+++ b/solution.py
@@ -35,11 +35,42 @@
         lax.all_gather(norm_second, "col", axis=0, tiled=True),
         lax.all_gather(router_weight, "col", axis=0, tiled=True),
     )
+
+    def joints_assign(z):
+        across = "row"
+        d_next = jax.lax.axis_size(across)
+        clean, base_arr, w2 = (d_next, jax.lax.axis_index(across), z.shape[1])
+        arrivals = []
+        nth = 0
+        while nth < clean:
+            arrivals.append((nth, (nth + 1) % clean))
+            nth += 1
+        made = []
+        nth = 0
+        while nth < clean:
+            made.append((nth, (nth - 1) % clean))
+            nth += 1
+        inter = jnp.zeros((*z.shape[:1], clean * w2, *z.shape[2:]), z.dtype)
+        inter = lax.dynamic_update_slice_in_dim(inter, z, base_arr * w2, axis=1)
+        y1 = block_now = z
+        mid_arr = clean // 2
+        m = 1
+        while m < mid_arr + 1:
+            y1 = jax.lax.ppermute(y1, across, arrivals)
+            inter = lax.dynamic_update_slice_in_dim(inter, y1, (base_arr - m) % clean * w2, axis=1)
+            if m < clean - mid_arr:
+                block_now = jax.lax.ppermute(block_now, across, made)
+                inter = lax.dynamic_update_slice_in_dim(
+                    inter, block_now, (base_arr + m) % clean * w2, axis=1
+                )
+            m = m + 1
+        return inter
+
     gathered = (
         lax.all_gather(col_pieces[0], "row", axis=0, tiled=True),
         lax.all_gather(col_pieces[1], "row", axis=1, tiled=True),
         lax.all_gather(col_pieces[2], "row", axis=0, tiled=True),
-        lax.all_gather(col_pieces[3], "row", axis=1, tiled=True),
+        joints_assign(col_pieces[3]),
         lax.all_gather(col_pieces[4], "row", axis=0, tiled=True),
         lax.all_gather(col_pieces[5], "row", axis=0, tiled=True),
         lax.all_gather(col_pieces[6], "row", axis=0, tiled=True),

time: 975 us -> 1190 us (1.22)
  blocking collectives: 78.4 us -> 203 us
  waiting for transfers between devices: 245 us -> 312 us
  local copies, waits for them, and re-layouts: 221 us -> 237 us
    all_gather x1, blocking collectives: 7.9 us -> 131 us  [local(): lax.all_gather(col_pieces[5], 'row', axis=0, tiled=True)]
    ppermute x0 -> x3, waiting for transfers between devices: none -> 61.8 us  [the longest x2 61.8 us: joints_assign(): y1 = jax.lax.ppermute(y1, across, arrivals)]
    all_gather x1, waiting for transfers between devices: 0.01 us -> 29.8 us  [local(): lax.all_gather(down_weight, 'col', axis=0, tiled=True)]
    reduce_scatter x1, waiting for transfers between devices: 86.9 us -> 59.8 us  [local(): lax.psum_scatter(down_part.astype(jnp.bfloat16), 'row', scatter_dimension...]
    reduce_scatter x1, waiting for transfers between devices: 60.6 us -> 86.9 us  [local(): lax.psum_scatter(up_part.astype(jnp.bfloat16), 'row', scatter_dimension=0...]
    all_gather x1, waiting for transfers between devices: 22.6 us -> 0.01 us  [local(): lax.all_gather(back_pieces[3], 'row', axis=1, tiled=True)]
    unnamed x86 -> x88, local copies, waits for them, and re-layouts: 70.9 us -> 70.8 us
  transfers between devices with their start and end apart: 15 -> 18, of which waited for: 6 -> 7; matrix products, arithmetic and copies ran while one was open for 55% -> 47% of each run, Pallas kernels for 0% -> 0%
where the time goes in v1:
time: 1190 us; the launch traced here: 1180 us
  waiting for transfers between devices  312 us (26%)
  local copies, waits for them, and re-layouts  237 us (20%)
  matrix products  225 us (19%)
  blocking collectives  203 us (17%)
  other arithmetic  176 us (15%)
  between operations  16.9 us (1%)
    all_gather x1, blocking collectives, local(): lax.all_gather(col_pieces[5], 'row', axis=0, tiled=True)  131 us
    reduce_scatter x1, waiting for transfers between devices, local(): lax.psum_scatter(up_part.astype(jnp.bfloat16), 'row', scatter_dimension=0...  86.9 us
    unnamed x88, local copies, waits for them, and re-layouts  70.8 us
    ppermute x2, waiting for transfers between devices, joints_assign(): y1 = jax.lax.ppermute(y1, across, arrivals)  61.8 us
    reduce_scatter x1, waiting for transfers between devices, local(): lax.psum_scatter(down_part.astype(jnp.bfloat16), 'row', scatter_dimension...  59.8 us
    scatter-add x1, other arithmetic, local(): input_grad = grad_out.at[token_rows].add(grad_picked)  39.5 us
    scatter-add x1, other arithmetic, local(): output = tokens.astype(jnp.float32).at[token_rows].add(gate_value[:, None...  39.3 us
    unnamed x3, blocking collectives  38.4 us
  transfers between devices with their start and end apart: 18, of which 7 were waited for; matrix products, arithmetic and copies ran while one was open for 47% of the time, Pallas kernels for 0%

profile of v1, /device:TPU:0, one launch (start us, length us, event | category | flops | bytes accessed | tf_op | source)
XLA Modules:
  0.0 1175.6 jit_solution(9891298022457914160)
XLA Ops:
  9.5 28.1 %all-gather.11.cloned.1.call-done = bf16[256,3072]{1,0:T(8,128)(2,1)} async-done(((bf16[256,384]{1,0:T(8,128)(2,1)}), bf16[256,3072]{1,0:T(8,128)(2,1)}) %all-gather.11.cloned.1.call-update) | async-done | bytes 1572880 | tf_op jit(solution)/shard_map/all_gather | solution.py:30
  68.9 29.8 %all-gather.21.cloned.1.call-done = bf16[4096,256]{1,0:T(8,128)(2,1)} async-done(((bf16[512,256]{1,0:T(8,128)(2,1)}), bf16[4096,256]{1,0:T(8,128)(2,1)}) %all-gather.21.cloned.1.call-update) | async-done | bytes 2097168 | tf_op jit(solution)/shard_map/all_gather | solution.py:33
  118.8 131.4 %all-gather.2 = bf16[4,1,256]{2,1,0:T(2,128)(2,1)S(1)} all-gather(bf16[1,1,256]{2,1,0:T(2,128)(2,1)S(1)} %reshape.157), channel_id=1, replica_groups=mesh['row'=4,'col'=8] {'row'}, dimensions={0}, use_global_device_ids=true | all-gather | bytes 2560 | tf_op jit(solution)/shard_map/all_gather | solution.py:75
  277.8 21.7 %convert_element_type.133 = f32[9216,1024]{1,0:T(8,128)} convert(bf16[9216,1024]{1,0:T(8,128)(2,1)} %param.19) | non-fusion elementwise | flops 9437184 | bytes 56623104 | tf_op jit(solution)/shard_map/convert_element_type | solution.py:136
  299.5 19.7 %gather_fusion.1 = f32[1152,1024]{1,0:T(8,128)} fusion(f32[9216,1024]{1,0:T(8,128)} %convert_element_type.133, s32[2048]{0:T(1024)S(1)} %pad_clamp_fusion), kind=kCustom, calls=%fused_computation.1 | custom fusion | bytes 9441792 | tf_op jit(solution)/shard_map/gather | solution.py:137
  350.5 61.8 %collective-permute-done.2 = bf16[4096,256]{1,0:T(8,128)(2,1)} collective-permute-done((bf16[4096,256]{1,0:T(8,128)(2,1)}, bf16[4096,256]{1,0:T(8,128)(2,1)}, u32[]{:S(2)}, u32[]{:S(2)}) %collective-permute-start.2) | collective-permute-done | bytes 2097184 | tf_op jit(solution)/shard_map/ppermute | solution.py:59
  428.2 30.2 %reshape.178 = bf16[9,128,16,3,64]{4,3,2,1,0:T(4,128)(2,1)} reshape(bf16[1152,3072]{1,0:T(8,128)(2,1)} %convolution_convert_fusion) | data formatting | bytes 14155776 | tf_op jit(solution)/shard_map/reshape | solution.py:90
  458.5 35.7 %fusion.63 = (bf16[9,128,16,1,64]{4,3,2,1,0:T(2,128)(2,1)}, bf16[9,128,16,1,64]{4,3,2,1,0:T(2,128)(2,1)}, bf16[9,128,16,1,64]{4,3,2,1,0:T(2,128)(2,1)}) fusion(bf16[9,128,16,3,64]{4,3,2,1,0:T(4,128)(2,1)} %reshape.178), kind=kLoop, calls=%fused_computation.110 | loop fusion | bytes 14155776 | tf_op jit(solution)/shard_map/slice | solution.py:93
  494.2 18.9 %copy.91 = bf16[9,128,16,1,64]{1,4,2,0,3:T(8,128)(2,1)S(1)} copy(bf16[9,128,16,1,64]{4,3,2,1,0:T(2,128)(2,1)} %get-tuple-element.25) | data formatting | bytes 4718592
  513.0 20.0 %copy.92 = bf16[9,128,16,1,64]{1,4,2,0,3:T(8,128)(2,1)} copy(bf16[9,128,16,1,64]{4,3,2,1,0:T(2,128)(2,1)} %get-tuple-element.26) | data formatting | bytes 4718592
  533.0 20.0 %copy.93 = bf16[9,128,16,1,64]{1,4,2,0,3:T(8,128)(2,1)} copy(bf16[9,128,16,1,64]{4,3,2,1,0:T(2,128)(2,1)} %get-tuple-element.27) | data formatting | bytes 4718592
  580.8 17.8 %fusion.62 = f32[1152,4096]{1,0:T(8,128)} fusion(bf16[1024,4096]{1,0:T(8,128)(2,1)} %all-gather.19.cloned.1.call-done, f32[1152,1024]{0,1:T(8,128)} %get-tuple-element.24, f32[1024]{0:T(1024)S(1)} %bitcast.110, f32[1152]{0:T(1024)S(1)} %get-tuple-element.34), kind=kOutput, calls=%fused_computation.109 | convolution fusion | flops 9667215360 | bytes 31990272 | tf_op jit(solution)/shard_map/dot_general | solution.py:113
  598.6 28.2 %fusion.6 = bf16[1152,4096]{1,0:T(8,128)(2,1)} fusion(f32[1152,4096]{1,0:T(8,128)} %fusion.62, bf16[4096,1024]{1,0:T(8,128)(2,1)} %all-gather.23.cloned.1.call-done, f32[1152,1024]{0,1:T(8,128)} %copy.65, f32[1152]{0:T(1024)S(1)} %add_divide_fusion), kind=kOutput, calls=%fused_computation.12 | convolution fusion | flops 9760407552 | bytes 41423360 | tf_op jit(solution)/shard_map/dot_general | solution.py:141
  626.8 19.3 %multiply_reduce_fusion.1 = (bf16[1024]{0:T(1024)(128)(2,1)}, f32[1152]{0:T(1024)S(1)}, f32[1152,1024]{0,1:T(8,128)}) fusion(f32[1152,1024]{0,1:T(8,128)} %get-tuple-element.24, f32[1152]{0:T(1024)S(1)} %get-tuple-element.34, f32[1024]{0:T(1024)S(1)} %bitcast.111, bf16[1152,4096]{1,0:T(8,128)(2,1)} %fusion.6, ...), kind=kOutput, calls=%fused_computation.50 | convolution fusion | flops 9670752256 | bytes 27278336 | tf_op jit(solution)/shard_map/dot_general | solution.py:145
  646.1 25.9 %multiply_reduce_fusion.2 = (f32[1152]{0:T(1024)}, f32[1152,1024]{0,1:T(8,128)}, bf16[1152,1024]{0,1:T(8,128)(2,1)}) fusion(f32[1152,1024]{0,1:T(8,128)} %copy.65, f32[1152]{0:T(1024)S(1)} %add_divide_fusion, f32[1152]{0:T(1024)S(1)} %get-tuple-element.10, f32[1152,1024]{0,1:T(8,128)} %get-tuple-element.24, f32[1152]{0:T(1024)S(1)} %get-tuple-element.33, ...), kind=kOutput, calls=%fused_computation.51 | convolution fusion | flops 9721478144 | bytes 53242368 | tf_op jit(solution)/shard_map/dot_general | solution.py:116
  760.4 17.9 %convolution_convert_fusion.2 = bf16[1024,4096]{1,0:T(8,128)(2,1)} fusion(bf16[1152,4096]{1,0:T(8,128)(2,1)} %fusion.6, f32[1152,1024]{0,1:T(8,128)} %get-tuple-element.24, f32[1024]{0:T(1024)S(1)} %bitcast.113, f32[1152]{0:T(1024)S(1)} %get-tuple-element.34), kind=kOutput, calls=%fused_computation.30 | convolution fusion | flops 9671409664 | bytes 22553088 | tf_op jit(solution)/shard_map/dot_general | solution.py:144
  778.4 21.9 %convolution_convert_fusion.1 = bf16[4096,1024]{1,0:T(8,128)(2,1)} fusion(f32[1152,1024]{0,1:T(8,128)} %copy.65, f32[1152]{0:T(1024)S(1)} %add_divide_fusion, f32[1152,4096]{1,0:T(8,128)} %fusion.62), kind=kOutput, calls=%fused_computation.29 | convolution fusion | flops 9712697344 | bytes 31986176 | tf_op jit(solution)/shard_map/dot_general | solution.py:142
  801.0 28.8 %reduce-scatter.11.cloned.1.call-done = bf16[256,3072]{1,0:T(8,128)(2,1)} async-done(((bf16[1024,3072]{1,0:T(8,128)(2,1)}), bf16[256,3072]{1,0:T(8,128)(2,1)}) %reduce-scatter.11.cloned.1.call-update) | async-done | bytes 1572880 | tf_op jit(solution)/shard_map/reduce_scatter | solution.py:194
  832.5 86.9 %reduce-scatter.17.cloned.1.call-done = bf16[256,4096]{1,0:T(8,128)(2,1)} async-done(((bf16[1024,4096]{1,0:T(8,128)(2,1)}), bf16[256,4096]{1,0:T(8,128)(2,1)}) %reduce-scatter.17.cloned.1.call-update) | async-done | bytes 2097168 | tf_op jit(solution)/shard_map/reduce_scatter | solution.py:200
  919.5 21.4 %convert_element_type.120 = f32[9216,1024]{1,0:T(8,128)} convert(bf16[9216,1024]{1,0:T(8,128)(2,1)} %param.10) | non-fusion elementwise | flops 9437184 | bytes 56623104 | tf_op jit(solution)/shard_map/convert_element_type | solution.py:119
  949.0 59.8 %reduce-scatter.21.cloned.1.call-done = bf16[4096,256]{1,0:T(8,128)(2,1)} async-done(((bf16[4096,1024]{1,0:T(8,128)(2,1)}), bf16[4096,256]{1,0:T(8,128)(2,1)}) %reduce-scatter.21.cloned.1.call-update) | async-done | bytes 2097168 | tf_op jit(solution)/shard_map/reduce_scatter | solution.py:203
  1036.9 39.5 %scatter_fusion.1 = f32[9216,1024]{1,0:T(8,128)} fusion(f32[9216,1024]{1,0:T(8,128)} %convert_element_type.133, s32[1152]{0:T(1024)S(1)} %copy-done.12, f32[1152,1024]{1,0:T(8,128)} %copy.76), kind=kCustom, calls=%fused_computation.3 | custom fusion | flops 1179648 | bytes 14160384 | tf_op jit(solution)/shard_map/scatter-add | solution.py:192
  1086.0 39.3 %scatter_fusion = f32[9216,1024]{1,0:T(8,128)} fusion(f32[9216,1024]{1,0:T(8,128)} %convert_element_type.120, s32[1152]{0:T(1024)S(1)} %copy-done.12, f32[1152,1024]{1,0:T(8,128)} %copy.64), kind=kCustom, calls=%fused_computation.2 | custom fusion | flops 1179648 | bytes 14160384 | tf_op jit(solution)/shard_map/scatter-add | solution.py:121
  1125.3 20.9 %convert_element_type.132 = bf16[9216,1024]{1,0:T(8,128)(2,1)} convert(f32[9216,1024]{1,0:T(8,128)} %scatter_fusion) | non-fusion elementwise | flops 9437184 | bytes 56623104 | tf_op jit(solution)/shard_map/convert_element_type | solution.py:122
  (189 shorter events, 313.4 us)
Async XLA Ops:
  7.2 94.8 %copy-start.29 = (u32[32]{0:T(128)S(1)}, u32[32]{0:T(128)}, u32[]{:S(2)}) copy-start(u32[32]{0:T(128)} %constant.78) | copy-start | bytes 388
  7.2 96.0 %copy-start.30 = (bf16[32]{0:T(256)(128)(2,1)S(1)}, bf16[32]{0:T(256)(128)(2,1)}, u32[]{:S(2)}) copy-start(bf16[32]{0:T(256)(128)(2,1)} %param.15) | copy-start | bytes 196
  7.2 96.2 %copy-start.31 = (bf16[32]{0:T(256)(128)(2,1)S(1)}, bf16[32]{0:T(256)(128)(2,1)}, u32[]{:S(2)}) copy-start(bf16[32]{0:T(256)(128)(2,1)} %param.12) | copy-start | bytes 196
  7.2 96.5 %copy-start.32 = (bf16[32]{0:T(256)(128)(2,1)S(1)}, bf16[32]{0:T(256)(128)(2,1)}, u32[]{:S(2)}) copy-start(bf16[32]{0:T(256)(128)(2,1)} %param.11) | copy-start | bytes 196
  7.2 30.4 %all-gather.11.cloned.1.call-start = ((), (), s32[]{:S(2)}) async-start(), calls=%async_computation.8 | async-start | bytes 1769472 | tf_op jit(solution)/shard_map/all_gather | solution.py:30
  8.0 60.9 %all-gather.17.cloned.1.call-start = ((), (), s32[]{:S(2)}) async-start(), calls=%async_computation.11 | async-start | bytes 2359296 | tf_op jit(solution)/shard_map/all_gather | solution.py:32
  8.7 90.0 %all-gather.21.cloned.1.call-start = ((), (), s32[]{:S(2)}) async-start(), calls=%async_computation.13 | async-start | bytes 2359296 | tf_op jit(solution)/shard_map/all_gather | solution.py:33
  9.4 406.0 %all-gather.13.cloned.1.call-start = ((), (), s32[]{:S(2)}) async-start(), calls=%async_computation.9 | async-start | bytes 7864320 | tf_op jit(solution)/shard_map/all_gather | solution.py:70
  37.7 532.9 %all-gather.15.cloned.1.call-start = ((), (), s32[]{:S(2)}) async-start(), calls=%async_computation.10 | async-start | bytes 2621440 | tf_op jit(solution)/shard_map/all_gather | solution.py:71
  54.7 526.1 %all-gather.19.cloned.1.call-start = ((), (), s32[]{:S(2)}) async-start(), calls=%async_computation.12 | async-start | bytes 10485760 | tf_op jit(solution)/shard_map/all_gather | solution.py:72
  68.9 529.7 %all-gather.23.cloned.1.call-start = ((), (), s32[]{:S(2)}) async-start(), calls=%async_computation.14 | async-start | bytes 10485760 | tf_op jit(solution)/shard_map/all_gather | solution.py:134
  98.8 236.4 %collective-permute-start = (bf16[4096,256]{1,0:T(8,128)(2,1)}, bf16[4096,256]{1,0:T(8,128)(2,1)}, u32[]{:S(2)}, u32[]{:S(2)}) collective-permute-start(bf16[4096,256]{1,0:T(8,128)(2,1)} %all-gather.21.cloned.1.call-done), channel_id=1, source_target_pairs={{0,8},{8,16},{16,24},{24,0},{1,9},{9,17},{17,25},{25,1},{2,10},{10... | collective-permute-start | bytes 6291464 | tf_op jit(solution)/shard_map/ppermute | solution.py:59
  100.3 247.0 %collective-permute-start.1 = (bf16[4096,256]{1,0:T(8,128)(2,1)}, bf16[4096,256]{1,0:T(8,128)(2,1)}, u32[]{:S(2)}, u32[]{:S(2)}) collective-permute-start(bf16[4096,256]{1,0:T(8,128)(2,1)} %all-gather.21.cloned.1.call-done), channel_id=1, source_target_pairs={{0,24},{8,0},{16,8},{24,16},{1,25},{9,1},{17,9},{25,17},{2,26},{10... | collective-permute-start | bytes 6291464 | tf_op jit(solution)/shard_map/ppermute | solution.py:62
  259.1 156.4 %copy-start.22 = (f32[4,1,256]{2,1,0:T(1,128)}, f32[4,1,256]{2,1,0:T(1,128)S(1)}, u32[]{:S(2)}) copy-start(f32[4,1,256]{2,1,0:T(1,128)S(1)} %convert_element_type.155) | copy-start | bytes 12292
  277.7 137.7 %copy-start.4 = (bf16[1152,1024]{0,1:T(8,128)(2,1)}, bf16[1152,1024]{0,1:T(8,128)(2,1)S(1)}, u32[]{:S(2)}) copy-start(bf16[1152,1024]{0,1:T(8,128)(2,1)S(1)} %copy.57) | copy-start | bytes 7077892
  335.7 76.6 %collective-permute-start.2 = (bf16[4096,256]{1,0:T(8,128)(2,1)}, bf16[4096,256]{1,0:T(8,128)(2,1)}, u32[]{:S(2)}, u32[]{:S(2)}) collective-permute-start(bf16[4096,256]{1,0:T(8,128)(2,1)} %collective-permute-done), channel_id=1, source_target_pairs={{0,8},{8,16},{16,24},{24,0},{1,9},{9,17},{17,25},{25,1},{2,10},{10... | collective-permute-start | bytes 6291464 | tf_op jit(solution)/shard_map/ppermute | solution.py:59
  338.4 462.1 %reduce-scatter.13.cloned.1.call-start = ((), (), s32[]{:S(2)}) async-start(), calls=%async_computation.16 | async-start | bytes 2621440 | tf_op jit(solution)/shard_map/reduce_scatter | solution.py:197
  679.2 150.5 %reduce-scatter.11.cloned.1.call-start = ((), (), s32[]{:S(2)}) async-start(), calls=%async_computation.15 | async-start | bytes 7864320 | tf_op jit(solution)/shard_map/reduce_scatter | solution.py:194
  760.4 159.0 %reduce-scatter.17.cloned.1.call-start = ((), (), s32[]{:S(2)}) async-start(), calls=%async_computation.18 | async-start | bytes 10485760 | tf_op jit(solution)/shard_map/reduce_scatter | solution.py:200
  778.4 230.4 %reduce-scatter.21.cloned.1.call-start = ((), (), s32[]{:S(2)}) async-start(), calls=%async_computation.20 | async-start | bytes 10485760 | tf_op jit(solution)/shard_map/reduce_scatter | solution.py:203
  800.4 361.3 %reduce-scatter.15.cloned.1.call-start = ((), (), s32[]{:S(2)}) async-start(), calls=%async_computation.17 | async-start | bytes 589824 | tf_op jit(solution)/shard_map/reduce_scatter | solution.py:220
  801.0 362.2 %reduce-scatter.25.cloned.1.call-start = ((), (), s32[]{:S(2)}) async-start(), calls=%async_computation.22 | async-start | bytes 1769472
  832.4 332.6 %reduce-scatter.19.cloned.1.call-start = ((), (), s32[]{:S(2)}) async-start(), calls=%async_computation.19 | async-start | bytes 2359296 | tf_op jit(solution)/shard_map/reduce_scatter | solution.py:223
  919.4 247.4 %reduce-scatter.23.cloned.1.call-start = ((), (), s32[]{:S(2)}) async-start(), calls=%async_computation.21 | async-start | bytes 2359296 | tf_op jit(solution)/shard_map/reduce_scatter | solution.py:226
  (28 other events, 623.1 us)
Sparse Core Ops, SparseCore 0:
  9.7 27.9 all-gather.10
  39.2 29.5 all-gather.16
  70.5 28.2 all-gather.20
  100.5 120.1 all-gather.12
  222.3 42.9 all-gather.14
  267.0 106.1 all-gather.18
  375.0 99.4 all-gather.22
  679.4 34.3 reduce-scatter.12
  760.5 69.2 reduce-scatter.10
  833.0 86.3 reduce-scatter.16
  922.5 86.3 reduce-scatter.20
  1011.0 30.8 reduce-scatter.14
  1044.2 32.4 reduce-scatter.24
  1078.9 33.7 reduce-scatter.18
  1114.8 34.5 reduce-scatter.22
